TPU v7x, 32 devices: a whole 2x2x4 slice. The times are simulated.
32 devices in a mesh: grp: 4 (over x, core), sec: 8 (over z, y).
Axes of the slice: x: 2, y: 2, z: 4, core: 2. Of those that a mesh axis runs over, the one named last changes fastest.
Arguments:
- trial: bfloat16 [2, 8, 256, 256], P(None, 'sec', 'grp'), may hold values from -6 to 6
- left_ops: bfloat16 [64, 8, 256, 256], P('grp', 'sec'), may hold values from -0.375 to 0.375
- right_ops: bfloat16 [64, 8, 256, 256], P('grp', 'sec'), may hold values from -0.046875 to 0.046875
- source: int32 [64, 8], P('grp', 'sec'), may hold values from 0 to 7
- live: int32 [64, 8], P('grp', 'sec'), may hold values 0 or 1
Outputs:
- sigma: bfloat16 [2, 8, 256, 256], P(None, 'sec', 'grp')
All inputs are finite; a program needn't handle non-finite values. No bound on the sum of `live` on one device may be relied on, other than what follows from the above.
Results may differ from a plain program's by a relative error of at most 0.0049.
Values may be sent and summed in bfloat16 or wider, within the bound.
No kernel may reach another device: no remote copies, remote signals or barrier semaphores. Data moves between devices by JAX's collectives and lax.ppermute only.
A program may use at most 64 MiB of HBM per device.

v0:
```python
import jax
import jax.numpy as jnp
from jax import lax
from jax.sharding import PartitionSpec as P


def body(trial, left_ops, right_ops, source, live):
    own_block = lax.all_gather(trial, "grp", axis=2, tiled=True)
    gathered = lax.all_gather(own_block, "sec", axis=1, tiled=True)
    picked = jnp.take(gathered, source[:, 0], axis=1)
    left = left_ops[:, 0]
    right = right_ops[:, 0]
    inner = jnp.einsum("kab,vkbc->vkac", left, picked, preferred_element_type=jnp.float32)
    inner = inner.astype(jnp.bfloat16) * live[:, 0].astype(jnp.bfloat16)[None, :, None, None]
    partial_value = jnp.einsum("vkac,kdc->vad", inner, right, preferred_element_type=jnp.float32)[
        :, None
    ]
    totals = lax.psum(partial_value, "grp")
    row_count = trial.shape[2]
    mine = lax.dynamic_slice_in_dim(totals, lax.axis_index("grp") * row_count, row_count, 2)
    return mine.astype(jnp.bfloat16)


def solution(mesh):
    in_specs = (
        P(None, "sec", "grp", None),
        P("grp", "sec", None, None),
        P("grp", "sec", None, None),
        P("grp", "sec"),
        P("grp", "sec"),
    )
    out_specs = P(None, "sec", "grp", None)
    return jax.shard_map(body, mesh=mesh, in_specs=in_specs, out_specs=out_specs, check_vma=False)
```

profile of v0, /device:TPU:0, one launch (start us, length us, event | category | flops | bytes accessed | tf_op | source)
XLA Modules:
  0.0 98.7 jit_solution(3914055519167033468)
XLA Ops:
  6.5 0.0 copy-start
  6.5 0.0 all-gather.2.cloned.1.call-start
  6.5 9.0 %all_gather.6 = bf16[2,1,256,256]{3,2,1,0:T(8,128)(2,1)} all-gather(bf16[2,1,64,256]{3,2,1,0:T(8,128)(2,1)} %param.5), channel_id=1, replica_groups=mesh['grp'=4,'sec'=8] {'grp'}, dimensions={2}, use_global_device_ids=true | all-gather | bytes 327680 | tf_op jit(solution)/shard_map/all_gather | solution.py:8
  15.5 0.0 all-gather.2.cloned.1.call-update
  15.5 0.7 fusion.24
  16.2 0.7 and_bitcast_fusion
  16.9 0.7 convert_bitcast_fusion
  17.5 47.6 %all-gather.2.cloned.1.call-done = bf16[2,8,256,256]{3,2,1,0:T(8,128)(2,1)} async-done(((bf16[2,1,256,256]{3,2,1,0:T(8,128)(2,1)}), bf16[2,8,256,256]{3,2,1,0:T(8,128)(2,1)}) %all-gather.2.cloned.1.call-update) | async-done | bytes 2097168 | tf_op jit(solution)/shard_map/all_gather | solution.py:9
  65.1 4.3 %gather_fusion = bf16[16,2,256,256]{3,2,1,0:T(8,128)(2,1)} fusion(bf16[2,8,256,256]{3,2,1,0:T(8,128)(2,1)} %all-gather.2.cloned.1.call-done, s32[1024]{0:T(1024)S(1)} %pad_clamp_fusion), kind=kCustom, calls=%fused_computation | custom fusion | bytes 8388672 | tf_op jit(solution)/shard_map/jit(_take)/gather | solution.py:10
  69.4 0.0 copy-done
  69.4 5.4 %fusion.14 = f32[2,1,256,256]{3,2,0,1:T(8,128)S(1)} fusion(bf16[16,1,256,256]{3,2,1,0:T(8,128)(2,1)S(1)} %copy-done, bf16[16,1,256,256]{3,2,1,0:T(8,128)(2,1)} %param.6, bf16[16]{0:T(256)(128)(2,1)S(1)} %convert_bitcast_fusion, bf16[16,2,256,256]{3,2,1,0:T(8,128)(2,1)} %gather_fusion, pred[16]{0:T(512)(128)(4,1)S(1)} %and_bitcast_fusion), kind=kOutput, calls=%fused_computation.11 | convolution fusion | flops 2153775104 | bytes 8912944 | tf_op jit(solution)/shard_map/vkac,kdc->vad/dot_general | solution.py:15
  74.8 16.4 %all-reduce.1 = bf16[2,1,256,256]{3,2,0,1:T(8,128)(2,1)S(1)} all-reduce(f32[2,1,256,256]{3,2,0,1:T(8,128)S(1)} %fusion.14), channel_id=1, replica_groups=mesh['grp'=4,'sec'=8] {'grp'}, use_global_device_ids=true, to_apply=%region_0.1 | all-reduce | flops 131072 | bytes 786432 | tf_op jit(solution)/shard_map/psum | solution.py:18
  91.2 0.6 fusion.23
  (1 shorter events, 0.0 us)
Async XLA Ops:
  6.5 62.9 %copy-start = (bf16[16,1,256,256]{3,2,1,0:T(8,128)(2,1)S(1)}, bf16[16,1,256,256]{3,2,1,0:T(8,128)(2,1)}, u32[]{:S(2)}) copy-start(bf16[16,1,256,256]{3,2,1,0:T(8,128)(2,1)} %param.7) | copy-start | bytes 6291460
  6.5 58.5 %all-gather.2.cloned.1.call-start = ((), (), s32[]{:S(2)}) async-start(), calls=%async_computation | async-start | bytes 2359296 | tf_op jit(solution)/shard_map/all_gather | solution.py:9
Sparse Core Ops, SparseCore 0:
  15.6 49.3 all-gather.1
where the time goes:
time: 98.9 us; the launch traced here: 98.7 us
  waiting for transfers between devices  47.6 us (48%)
  blocking collectives  25.3 us (26%)
  between operations  13.4 us (14%)
  matrix products  5.39 us (5%)
  local copies, waits for them, and re-layouts  4.98 us (5%)
  other arithmetic  1.99 us (2%)
    all_gather x1, waiting for transfers between devices, body(): gathered = lax.all_gather(own_block, 'sec', axis=1, tiled=True)  47.6 us
    psum x1, blocking collectives, body(): totals = lax.psum(partial_value, 'grp')  16.4 us
    all_gather x1, blocking collectives, body(): own_block = lax.all_gather(trial, 'grp', axis=2, tiled=True)  8.95 us
    dot_general x1, matrix products, body(): jnp.einsum('vkac,kdc->vad', inner, right, preferred_element_type=jnp.floa...  5.39 us
    gather x1, local copies, waits for them, and re-layouts, body(): picked = jnp.take(gathered, source[:, 0], axis=1)  4.34 us
  transfers between devices with their start and end apart: 1, of which 1 were waited for; matrix products, arithmetic and copies ran while one was open for 2% of the time, Pallas kernels for 0%

commit v1 on v0

--- a/solution.py
+++ b/solution.py
@@ -15,7 +15,7 @@
     partial_value = jnp.einsum("vkac,kdc->vad", inner, right, preferred_element_type=jnp.float32)[
         :, None
     ]
-    totals = lax.psum(partial_value, "grp")
+    totals = jnp.sum(lax.all_gather(partial_value, "grp"), axis=0)
     row_count = trial.shape[2]
     mine = lax.dynamic_slice_in_dim(totals, lax.axis_index("grp") * row_count, row_count, 2)
     return mine.astype(jnp.bfloat16)

time: 98.9 us -> 106 us (1.072)
  waiting for transfers between devices: 47.6 us -> 68.8 us
  blocking collectives: 25.3 us -> 8.95 us
  other arithmetic: 1.99 us -> 3.73 us
    all_gather x0 -> x1, waiting for transfers between devices: none -> 21.2 us  [body(): totals = jnp.sum(lax.all_gather(partial_value, 'grp'), axis=0)]
    psum x1 -> x0, blocking collectives: 16.4 us -> none  [body(): totals = lax.psum(partial_value, 'grp')]
    reduce_sum x0 -> x1, other arithmetic: none -> 1.75 us  [body(): totals = jnp.sum(lax.all_gather(partial_value, 'grp'), axis=0)]
  transfers between devices with their start and end apart: 1 -> 2, of which waited for: 1 -> 2; matrix products, arithmetic and copies ran while one was open for 2% -> 2% of each run, Pallas kernels for 0% -> 0%
where the time goes in v1:
time: 106 us
  waiting for transfers between devices  68.8 us (65%)
  between operations  13.4 us (13%)
  blocking collectives  8.95 us (8%)
  matrix products  6.2 us (6%)
  local copies, waits for them, and re-layouts  4.99 us (5%)
  other arithmetic  3.73 us (4%)
    all_gather x1, waiting for transfers between devices, body(): gathered = lax.all_gather(own_block, 'sec', axis=1, tiled=True)  47.5 us
    all_gather x1, waiting for transfers between devices, body(): totals = jnp.sum(lax.all_gather(partial_value, 'grp'), axis=0)  21.2 us
    all_gather x1, blocking collectives, body(): own_block = lax.all_gather(trial, 'grp', axis=2, tiled=True)  8.95 us
    dot_general x1, matrix products, body(): jnp.einsum('vkac,kdc->vad', inner, right, preferred_element_type=jnp.floa...  6.2 us
    gather x1, local copies, waits for them, and re-layouts, body(): picked = jnp.take(gathered, source[:, 0], axis=1)  4.34 us
  transfers between devices with their start and end apart: 2, of which 2 were waited for; matrix products, arithmetic and copies ran while one was open for 2% of the time, Pallas kernels for 0%

profile of v1, /device:TPU:0, one launch (start us, length us, event | category | flops | bytes accessed | tf_op | source)
XLA Modules:
  0.0 106.1 jit_solution(2665293806132851209)
XLA Ops:
  6.5 0.0 copy-start
  6.5 0.0 all-gather.4.cloned.1.call-start
  6.5 9.0 %all_gather.9 = bf16[2,1,256,256]{3,2,1,0:T(8,128)(2,1)} all-gather(bf16[2,1,64,256]{3,2,1,0:T(8,128)(2,1)} %param.5), channel_id=1, replica_groups=mesh['grp'=4,'sec'=8] {'grp'}, dimensions={2}, use_global_device_ids=true | all-gather | bytes 327680 | tf_op jit(solution)/shard_map/all_gather | solution.py:8
  15.5 0.0 all-gather.4.cloned.1.call-update
  15.5 0.0 all-gather.6.cloned.1.call-start
  15.6 0.7 fusion.24
  16.2 0.7 and_bitcast_fusion
  16.9 0.7 convert_bitcast_fusion
  17.6 47.5 %all-gather.4.cloned.1.call-done = bf16[2,8,256,256]{3,2,1,0:T(8,128)(2,1)} async-done(((bf16[2,1,256,256]{3,2,1,0:T(8,128)(2,1)}), bf16[2,8,256,256]{3,2,1,0:T(8,128)(2,1)}) %all-gather.4.cloned.1.call-update) | async-done | bytes 2097168 | tf_op jit(solution)/shard_map/all_gather | solution.py:9
  65.1 4.3 %gather_fusion = bf16[16,2,256,256]{3,2,1,0:T(8,128)(2,1)} fusion(bf16[2,8,256,256]{3,2,1,0:T(8,128)(2,1)} %all-gather.4.cloned.1.call-done, s32[1024]{0:T(1024)S(1)} %pad_clamp_fusion), kind=kCustom, calls=%fused_computation | custom fusion | bytes 8388672 | tf_op jit(solution)/shard_map/jit(_take)/gather | solution.py:10
  69.4 0.0 copy-done
  69.4 6.2 %fusion.14 = f32[2,256,256]{2,1,0:T(8,128)} fusion(bf16[16,1,256,256]{3,2,1,0:T(8,128)(2,1)S(1)} %copy-done, bf16[16,1,256,256]{3,2,1,0:T(8,128)(2,1)} %param.6, bf16[16]{0:T(256)(128)(2,1)S(1)} %convert_bitcast_fusion, bf16[16,2,256,256]{3,2,1,0:T(8,128)(2,1)} %gather_fusion, pred[16]{0:T(512)(128)(4,1)S(1)} %and_bitcast_fusion), kind=kOutput, calls=%fused_computation.11 | convolution fusion | flops 2153775104 | bytes 8912944 | tf_op jit(solution)/shard_map/vkac,kdc->vad/dot_general | solution.py:15
  75.6 0.0 all-gather.6.cloned.1.call-update
  75.6 21.2 %all-gather.6.cloned.1.call-done = f32[8,256,256]{2,1,0:T(8,128)} async-done(((f32[2,256,256]{2,1,0:T(8,128)}), f32[8,256,256]{2,1,0:T(8,128)}) %all-gather.6.cloned.1.call-update) | async-done | bytes 2097168 | tf_op jit(solution)/shard_map/all_gather | solution.py:18
  96.9 1.7 %reduce.1 = bf16[2,256,256]{2,1,0:T(8,128)(2,1)S(1)} reduce(f32[4,2,256,256]{3,2,1,0:T(8,128)} %bitcast.35, f32[]{:T(128)} %constant.24.clone.1), dimensions={0}, to_apply=%region_0.1 | reduce | flops 393216 | bytes 2359300 | tf_op jit(solution)/shard_map/reduce_sum | solution.py:18
  98.6 0.6 fusion.23
  (1 shorter events, 0.0 us)
Async XLA Ops:
  6.5 62.9 %copy-start = (bf16[16,1,256,256]{3,2,1,0:T(8,128)(2,1)S(1)}, bf16[16,1,256,256]{3,2,1,0:T(8,128)(2,1)}, u32[]{:S(2)}) copy-start(bf16[16,1,256,256]{3,2,1,0:T(8,128)(2,1)} %param.7) | copy-start | bytes 6291460
  6.5 58.5 %all-gather.4.cloned.1.call-start = ((), (), s32[]{:S(2)}) async-start(), calls=%async_computation | async-start | bytes 2359296 | tf_op jit(solution)/shard_map/all_gather | solution.py:9
  15.5 81.4 %all-gather.6.cloned.1.call-start = ((), (), s32[]{:S(2)}) async-start(), calls=%async_computation.1 | async-start | bytes 2621440 | tf_op jit(solution)/shard_map/all_gather | solution.py:18
Sparse Core Ops, SparseCore 0:
  15.6 49.3 all-gather.3
  75.8 21.0 all-gather.5
